TPU v7x, 32 devices: a whole 2x2x4 slice. The times are simulated.
32 devices in a mesh: dp: 4 (over z), tensor: 8 (over y, x, core).
Axes of the slice: x: 2, y: 2, z: 4, core: 2. Of those that a mesh axis runs over, the one named last changes fastest.
Arguments:
- activations: bfloat16 [3072, 4096], P('dp', 'tensor'), may hold values from -6 to 6
- out_grads_t: bfloat16 [5504, 3072], P('tensor', 'dp'), may hold values from -6 to 6
- in_basis: bfloat16 [4096, 4096], P(None, 'tensor'), may hold values from -0.09375 to 0.09375
- out_basis_t: bfloat16 [5504, 5504], P('tensor'), may hold values from -0.078125 to 0.078125
- query_proj: bfloat16 [4, 5504, 4096], P(None, 'tensor', 'dp'), may hold values from -6 to 6
- eigvals: float32 [5504, 4096], P('tensor', 'dp'), may hold values from 0.05 to 5
- damping: float32 [1], replicated, may hold values from 0.05 to 0.2
- lengths: int32 [24], P('dp'), may hold values from 1 to 128, 1920 in all
Outputs:
- scores: float32 [24, 4], P('dp')
Inputs may be any that keep to these rules, and one draw needn't show every extreme that they name: `lengths`: the largest token count is exactly 128.
All inputs are finite; a program needn't handle non-finite values. No bound on the sum of `lengths` on one device may be relied on, other than what follows from the above.
Results may differ from a plain program's by a relative error of at most 0.006.
Values may be sent and summed in bfloat16 or wider, within the bound.
A program may use at most 128 MiB of HBM per device.

v0:
```python
import jax
import jax.numpy as jnp
from jax import lax
from jax.sharding import PartitionSpec as P


def local(activations, out_grads_t, in_basis, out_basis_t, query_proj, eigvals, damping, lengths):
    full_act = lax.all_gather(activations, "tensor", axis=1, tiled=True)
    act_local = jnp.dot(full_act, in_basis, preferred_element_type=jnp.float32).astype(jnp.bfloat16)
    act_proj = lax.all_gather(act_local, "tensor", axis=1, tiled=True)
    token_rows = full_act.shape[0]
    width = out_basis_t.shape[0]
    grad_full = jnp.dot(
        out_basis_t,
        lax.all_gather(out_grads_t, "tensor", axis=0, tiled=True),
        preferred_element_type=jnp.float32,
    )
    seq_count = lengths.shape[0]
    seq_len = token_rows // seq_count
    position = lax.broadcasted_iota(jnp.int32, (seq_count, seq_len), 1)
    keep = (position < lengths[:, None]).astype(jnp.float32).reshape(1, token_rows)
    grad_proj = (grad_full * keep).astype(jnp.bfloat16)
    scaled = (query_proj.astype(jnp.float32) / (eigvals + damping[0])).astype(jnp.bfloat16)
    query_count = query_proj.shape[0]
    mixed = jnp.einsum(
        "td,qjd->qjt",
        act_proj,
        lax.all_gather(scaled, "dp", axis=2, tiled=True),
        preferred_element_type=jnp.float32,
    )
    weighted = mixed * grad_proj.astype(jnp.float32)[None, :, :]
    partial_value = jnp.sum(weighted.reshape(query_count, width, seq_count, seq_len), axis=(1, 3)).T
    totals = lax.psum(partial_value, "tensor")
    norm_factor = (act_proj.shape[1] * out_basis_t.shape[1] * seq_len) ** (-0.5)
    return totals * norm_factor


def solution(mesh):
    placed = (
        P("dp", "tensor"),
        P("tensor", "dp"),
        P(None, "tensor"),
        P("tensor", None),
        P(None, "tensor", "dp"),
        P("tensor", "dp"),
        P(),
        P("dp"),
    )
    return jax.shard_map(
        local, mesh=mesh, in_specs=placed, out_specs=P("dp", None), check_vma=False
    )
```

profile of v0, /device:TPU:0, one launch (start us, length us, event | category | flops | bytes accessed | tf_op | source)
XLA Modules:
  0.0 591.1 jit_solution(7677577895891891836)
XLA Ops:
  6.5 0.7 all-gather.7.cloned.1.call-update
  7.3 0.0 all-gather.11.cloned.1.call-start
  7.3 0.7 all-gather.11.cloned.1.call-update
  8.0 0.0 copy-start
  8.0 0.0 all-gather.9.cloned.1.call-start
  8.1 50.5 %all-gather.7.cloned.1.call-done = bf16[768,4096]{1,0:T(8,128)(2,1)} async-done(((bf16[768,512]{1,0:T(8,128)(2,1)}), bf16[768,4096]{1,0:T(8,128)(2,1)}) %all-gather.7.cloned.1.call-update) | async-done | bytes 6291472 | tf_op jit(solution)/shard_map/all_gather | solution.py:8
  58.5 8.3 %convolution_convert_fusion = bf16[768,512]{1,0:T(8,128)(2,1)} fusion(bf16[768,4096]{1,0:T(8,128)(2,1)} %all-gather.7.cloned.1.call-done, bf16[4096,512]{1,0:T(8,128)(2,1)} %param.10), kind=kOutput, calls=%fused_computation.7 | convolution fusion | flops 3221618688 | bytes 11272192 | tf_op jit(solution)/shard_map/dot_general | solution.py:9
  66.9 0.0 all-gather.9.cloned.1.call-update
  66.9 0.0 all-gather.5.cloned.1.call-start
  67.6 0.0 copy-done
  67.6 0.5 broadcast_add_fusion
  68.1 0.0 copy-start.1
  68.1 7.5 %divide_convert_fusion = bf16[4,688,1024]{2,1,0:T(8,128)(2,1)} fusion(bf16[4,688,1024]{2,1,0:T(8,128)(2,1)} %param.12, f32[688,1024]{1,0:T(8,128)S(1)} %broadcast_add_fusion), kind=kLoop, calls=%fused_computation | loop fusion | flops 8454144 | bytes 14090240 | tf_op jit(solution)/shard_map/convert_element_type | solution.py:23
  75.6 0.0 all-gather.5.cloned.1.call-update
  75.6 0.0 copy-done.1
  75.6 0.1 convert_bitcast_fusion
  75.7 39.3 %all-gather.11.cloned.1.call-done = bf16[5504,768]{1,0:T(8,128)(2,1)} async-done(((bf16[688,768]{1,0:T(8,128)(2,1)}), bf16[5504,768]{1,0:T(8,128)(2,1)}) %all-gather.11.cloned.1.call-update) | async-done | bytes 8454160 | tf_op jit(solution)/shard_map/all_gather | solution.py:15
  115.0 10.9 %fusion.4 = f32[688,768]{1,0:T(8,128)S(1)} fusion(bf16[688,5504]{1,0:T(8,128)(2,1)} %param.11, bf16[5504,768]{1,0:T(8,128)(2,1)} %all-gather.11.cloned.1.call-done, f32[768]{0:T(1024)S(1)} %convert_bitcast_fusion), kind=kOutput, calls=%fused_computation.5 | convolution fusion | flops 5818036224 | bytes 18144256 | tf_op jit(solution)/shard_map/dot_general | solution.py:13
  125.9 37.6 %all-gather.9.cloned.1.call-done = bf16[768,4096]{1,0:T(8,128)(2,1)} async-done(((bf16[768,512]{1,0:T(8,128)(2,1)}), bf16[768,4096]{1,0:T(8,128)(2,1)}) %all-gather.9.cloned.1.call-update) | async-done | bytes 6291472 | tf_op jit(solution)/shard_map/all_gather | solution.py:10
  163.5 384.0 %all-gather.5.cloned.1.call-done = bf16[4,688,4096]{2,1,0:T(8,128)(2,1)} async-done(((bf16[4,688,1024]{2,1,0:T(8,128)(2,1)}), bf16[4,688,4096]{2,1,0:T(8,128)(2,1)}) %all-gather.5.cloned.1.call-update) | async-done | bytes 22544400 | tf_op jit(solution)/shard_map/all_gather | solution.py:28
  547.5 22.8 %multiply_reduce_fusion = f32[4,768]{1,0:T(4,128)S(1)} fusion(f32[688,768]{1,0:T(8,128)S(1)} %fusion.4, bf16[4,688,4096]{2,1,0:T(8,128)(2,1)} %all-gather.5.cloned.1.call-done, bf16[768,4096]{1,0:T(8,128)(2,1)} %all-gather.9.cloned.1.call-done), kind=kOutput, calls=%fused_computation.1 | convolution fusion | flops 17318309888 | bytes 30961664 | tf_op jit(solution)/shard_map/td,qjd->qjt/dot_general | solution.py:25
  570.3 0.1 reduce_sum.18
  570.4 13.6 %psum.7 = f32[6,4]{0,1:T(4,128)S(1)} all-reduce(f32[6,4]{0,1:T(4,128)S(1)} %bitcast.15), channel_id=1, replica_groups=mesh['dp'=4,'tensor'=8] {'tensor'}, use_global_device_ids=true, to_apply=%region_2.3 | all-reduce | flops 24 | bytes 192 | tf_op jit(solution)/shard_map/psum | solution.py:33
  584.0 0.6 broadcast_multiply_fusion
  (2 shorter events, 0.0 us)
Async XLA Ops:
  6.5 52.0 %all-gather.7.cloned.1.call-start = ((), (), s32[]{:S(2)}) async-start(), calls=%async_computation.1 | async-start | bytes 7077888 | tf_op jit(solution)/shard_map/all_gather | solution.py:8
  7.3 107.7 %all-gather.11.cloned.1.call-start = ((), (), s32[]{:S(2)}) async-start(), calls=%async_computation.3 | async-start | bytes 9510912 | tf_op jit(solution)/shard_map/all_gather | solution.py:15
  8.0 59.6 %copy-start = (f32[688,1024]{1,0:T(8,128)S(1)}, f32[688,1024]{1,0:T(8,128)}, u32[]{:S(2)}) copy-start(f32[688,1024]{1,0:T(8,128)} %param.13) | copy-start | bytes 8454148
  8.0 155.5 %all-gather.9.cloned.1.call-start = ((), (), s32[]{:S(2)}) async-start(), calls=%async_computation.2 | async-start | bytes 7077888 | tf_op jit(solution)/shard_map/all_gather | solution.py:10
  66.9 480.6 %all-gather.5.cloned.1.call-start = ((), (), s32[]{:S(2)}) async-start(), calls=%async_computation | async-start | bytes 28180480 | tf_op jit(solution)/shard_map/all_gather | solution.py:28
  68.1 7.5 %copy-start.1 = (s32[6]{0:T(128)S(1)}, s32[6]{0:T(128)}, u32[]{:S(2)}) copy-start(s32[6]{0:T(128)} %param.15) | copy-start | bytes 76
Sparse Core Ops, SparseCore 0:
  9.2 49.2 all-gather.6
  60.4 54.5 all-gather.10
  116.9 46.5 all-gather.8
  164.9 382.4 all-gather.4
where the time goes:
time: 591 us
  waiting for transfers between devices  513 us (87%)
  matrix products  42 us (7%)
  between operations  13.8 us (2%)
  blocking collectives  13.6 us (2%)
  other arithmetic  8.66 us (1%)
    all_gather x1, waiting for transfers between devices, local(): lax.all_gather(scaled, 'dp', axis=2, tiled=True)  384 us
    all_gather x1, waiting for transfers between devices, local(): full_act = lax.all_gather(activations, 'tensor', axis=1, tiled=True)  50.5 us
    all_gather x1, waiting for transfers between devices, local(): lax.all_gather(out_grads_t, 'tensor', axis=0, tiled=True)  39.3 us
    all_gather x1, waiting for transfers between devices, local(): act_proj = lax.all_gather(act_local, 'tensor', axis=1, tiled=True)  37.6 us
    dot_general x1, matrix products, local(): jnp.einsum('td,qjd->qjt', act_proj, lax.all_gather(scaled, 'dp', axis=2,...  22.8 us
    psum x1, blocking collectives, local(): totals = lax.psum(partial_value, 'tensor')  13.6 us
  transfers between devices with their start and end apart: 4, of which 4 were waited for; matrix products, arithmetic and copies ran while one was open for 5% of the time, Pallas kernels for 0%

commit v1 on v0

--- a/solution.py
+++ b/solution.py
@@ -22,12 +22,37 @@
     grad_proj = (grad_full * keep).astype(jnp.bfloat16)
     scaled = (query_proj.astype(jnp.float32) / (eigvals + damping[0])).astype(jnp.bfloat16)
     query_count = query_proj.shape[0]
+    size, position_2, span = (lax.axis_size("dp"), lax.axis_index("dp"), scaled.shape[2])
+    right = [(i, (i + 1) % size) for i in range(size)]
+    downward = [(i, (i - 1) % size) for i in range(size)]
+    middle = size // 2
+    from_left = from_right = scaled
     mixed = jnp.einsum(
         "td,qjd->qjt",
-        act_proj,
-        lax.all_gather(scaled, "dp", axis=2, tiled=True),
+        lax.dynamic_slice_in_dim(act_proj, position_2 * span, scaled.shape[2], axis=1),
+        scaled,
         preferred_element_type=jnp.float32,
     )
+    for step in range(1, middle + 1):
+        from_left = lax.ppermute(from_left, "dp", right)
+        if step < size - middle:
+            from_right = lax.ppermute(from_right, "dp", downward)
+            mixed = mixed + jnp.einsum(
+                "td,qjd->qjt",
+                lax.dynamic_slice_in_dim(
+                    act_proj, (position_2 + step) % size * span, from_right.shape[2], axis=1
+                ),
+                from_right,
+                preferred_element_type=jnp.float32,
+            )
+        mixed = mixed + jnp.einsum(
+            "td,qjd->qjt",
+            lax.dynamic_slice_in_dim(
+                act_proj, (position_2 - step) % size * span, from_left.shape[2], axis=1
+            ),
+            from_left,
+            preferred_element_type=jnp.float32,
+        )
     weighted = mixed * grad_proj.astype(jnp.float32)[None, :, :]
     partial_value = jnp.sum(weighted.reshape(query_count, width, seq_count, seq_len), axis=(1, 3)).T
     totals = lax.psum(partial_value, "tensor")

time: 591 us -> 479 us (0.81)
  waiting for transfers between devices: 513 us -> 375 us
  matrix products: 42 us -> 64.8 us
    all_gather x1 -> x0, waiting for transfers between devices: 384 us -> none  [local(): lax.all_gather(scaled, 'dp', axis=2, tiled=True)]
    ppermute x0 -> x3, waiting for transfers between devices: none -> 323 us  [the longest x2 235 us: local(): from_left = lax.ppermute(from_left, 'dp', right)]
    all_gather x1, waiting for transfers between devices: 39.3 us -> 0.01 us  [local(): lax.all_gather(out_grads_t, 'tensor', axis=0, tiled=True)]
    all_gather x1, waiting for transfers between devices: 37.6 us -> 0.02 us  [local(): act_proj = lax.all_gather(act_local, 'tensor', axis=1, tiled=True)]
    dot_general x1 -> x4, matrix products: 22.8 us -> 45.6 us  [the longest x3 36.3 us: local(): jnp.einsum('td,qjd->qjt', lax.dynamic_slice_in_dim(act_proj, (position_2...]
  transfers between devices with their start and end apart: 4 -> 6, of which waited for: 4 -> 4; matrix products, arithmetic and copies ran while one was open for 5% -> 12% of each run, Pallas kernels for 0% -> 0%
where the time goes in v1:
time: 479 us; the launch traced here: 478 us
  waiting for transfers between devices  375 us (78%)
  matrix products  64.8 us (14%)
  between operations  13.8 us (3%)
  blocking collectives  12.3 us (3%)
  other arithmetic  8.72 us (2%)
    ppermute x2, waiting for transfers between devices, local(): from_left = lax.ppermute(from_left, 'dp', right)  235 us
    ppermute x1, waiting for transfers between devices, local(): from_right = lax.ppermute(from_right, 'dp', downward)  88.3 us
    all_gather x1, waiting for transfers between devices, local(): full_act = lax.all_gather(activations, 'tensor', axis=1, tiled=True)  50.5 us
    dot_general x3, matrix products, local(): jnp.einsum('td,qjd->qjt', lax.dynamic_slice_in_dim(act_proj, (position_2...  36.3 us
    psum x1, blocking collectives, local(): totals = lax.psum(partial_value, 'tensor')  12.3 us
    dot_general x1, matrix products, local(): jnp.dot(out_basis_t, lax.all_gather(out_grads_t, 'tensor', axis=0, tiled=...  10.9 us
  transfers between devices with their start and end apart: 6, of which 4 were waited for; matrix products, arithmetic and copies ran while one was open for 12% of the time, Pallas kernels for 0%

profile of v1, /device:TPU:0, one launch (start us, length us, event | category | flops | bytes accessed | tf_op | source)
XLA Modules:
  0.0 478.4 jit_solution(1382612305699786052)
XLA Ops:
  6.5 0.7 all-gather.4.cloned.1.call-update
  7.3 0.0 all-gather.8.cloned.1.call-start
  7.3 0.7 all-gather.8.cloned.1.call-update
  8.0 0.0 all-gather.6.cloned.1.call-start
  8.1 50.5 %all-gather.4.cloned.1.call-done = bf16[768,4096]{1,0:T(8,128)(2,1)} async-done(((bf16[768,512]{1,0:T(8,128)(2,1)}), bf16[768,4096]{1,0:T(8,128)(2,1)}) %all-gather.4.cloned.1.call-update) | async-done | bytes 6291472 | tf_op jit(solution)/shard_map/all_gather | solution.py:8
  58.5 8.3 %convolution_convert_fusion = bf16[768,512]{1,0:T(8,128)(2,1)} fusion(bf16[768,4096]{1,0:T(8,128)(2,1)} %all-gather.4.cloned.1.call-done, bf16[4096,512]{1,0:T(8,128)(2,1)} %param.10), kind=kOutput, calls=%fused_computation.16 | convolution fusion | flops 3221618688 | bytes 11272192 | tf_op jit(solution)/shard_map/dot_general | solution.py:9
  66.8 0.0 all-gather.6.cloned.1.call-update
  67.5 0.5 broadcast_add_fusion
  68.0 7.5 %divide_convert_fusion = bf16[4,688,1024]{2,1,0:T(8,128)(2,1)} fusion(bf16[4,688,1024]{2,1,0:T(8,128)(2,1)} %param.12, f32[688,1024]{1,0:T(8,128)S(1)} %broadcast_add_fusion), kind=kLoop, calls=%fused_computation | loop fusion | flops 8454144 | bytes 14090240 | tf_op jit(solution)/shard_map/convert_element_type | solution.py:23
  75.5 1.6 collective-permute-start.1
  77.1 2.2 collective-permute-start
  79.3 122.7 %collective-permute-done.1 = bf16[4,688,1024]{2,1,0:T(8,128)(2,1)} collective-permute-done((bf16[4,688,1024]{2,1,0:T(8,128)(2,1)}, bf16[4,688,1024]{2,1,0:T(8,128)(2,1)}, u32[]{:S(2)}, u32[]{:S(2)}) %collective-permute-start.1) | collective-permute-done | bytes 5636128 | tf_op jit(solution)/shard_map/ppermute | solution.py:37
  202.0 0.1 convert_bitcast_fusion
  202.1 10.9 %fusion.11 = f32[688,768]{1,0:T(8,128)S(1)} fusion(bf16[688,5504]{1,0:T(8,128)(2,1)} %param.11, bf16[5504,768]{1,0:T(8,128)(2,1)} %all-gather.8.cloned.1.call-done, f32[768]{0:T(1024)S(1)} %convert_bitcast_fusion), kind=kOutput, calls=%fused_computation.14 | convolution fusion | flops 5818036224 | bytes 18144256 | tf_op jit(solution)/shard_map/dot_general | solution.py:13
  213.0 0.0 all-gather.6.cloned.1.call-done
  213.1 11.1 %fusion.1 = f32[4,688,768]{2,1,0:T(8,128)} fusion(bf16[4,688,1024]{2,1,0:T(8,128)(2,1)} %collective-permute-done.1, bf16[768,4096]{1,0:T(8,128)(2,1)} %all-gather.6.cloned.1.call-done, s32[]{:T(128)S(6)} %select_n.31), kind=kOutput, calls=%fused_computation.4 | convolution fusion | flops 4328521728 | bytes 15663108 | tf_op jit(solution)/shard_map/td,qjd->qjt/dot_general | solution.py:48
  224.1 9.2 %fusion.5 = f32[4,688,768]{2,1,0:T(8,128)} fusion(bf16[4,688,1024]{2,1,0:T(8,128)(2,1)} %divide_convert_fusion, bf16[768,4096]{1,0:T(8,128)(2,1)S(1)} %copy-done.2, s32[]{:T(128)S(6)} %select_n.27), kind=kOutput, calls=%fused_computation.8 | convolution fusion | flops 4328521728 | bytes 15663108 | tf_op jit(solution)/shard_map/td,qjd->qjt/dot_general | solution.py:30
  233.4 88.3 %collective-permute-done = bf16[4,688,1024]{2,1,0:T(8,128)(2,1)} collective-permute-done((bf16[4,688,1024]{2,1,0:T(8,128)(2,1)}, bf16[4,688,1024]{2,1,0:T(8,128)(2,1)}, u32[]{:S(2)}, u32[]{:S(2)}) %collective-permute-start) | collective-permute-done | bytes 5636128 | tf_op jit(solution)/shard_map/ppermute | solution.py:39
  321.6 9.3 %fusion.3 = f32[4,688,768]{2,1,0:T(8,128)} fusion(bf16[4,688,1024]{2,1,0:T(8,128)(2,1)} %collective-permute-done, bf16[768,4096]{1,0:T(8,128)(2,1)S(1)} %copy-done.2, s32[]{:T(128)S(6)} %select_n.29), kind=kOutput, calls=%fused_computation.6 | convolution fusion | flops 4328521728 | bytes 15663108 | tf_op jit(solution)/shard_map/td,qjd->qjt/dot_general | solution.py:40
  331.0 111.9 %collective-permute-done.2 = bf16[4,688,1024]{2,1,0:T(8,128)(2,1)} collective-permute-done((bf16[4,688,1024]{2,1,0:T(8,128)(2,1)}, bf16[4,688,1024]{2,1,0:T(8,128)(2,1)}, u32[]{:S(2)}, u32[]{:S(2)}) %collective-permute-start.2) | collective-permute-done | bytes 5636128 | tf_op jit(solution)/shard_map/ppermute | solution.py:37
  442.9 16.0 %multiply_reduce_fusion = f32[4,768]{1,0:T(4,128)S(1)} fusion(f32[4,688,768]{2,1,0:T(8,128)} %fusion.1, f32[4,688,768]{2,1,0:T(8,128)} %fusion.5, f32[4,688,768]{2,1,0:T(8,128)} %fusion.3, f32[688,768]{1,0:T(8,128)S(1)} %fusion.11, bf16[4,688,1024]{2,1,0:T(8,128)(2,1)} %collective-permute-done.2, bf16[768,4096]{1,0:T(8,128)(2,1)} %all-gather.6.cloned.1.call-done, ...), kind=kOutput, calls=%fused_computation.1 | convolution fusion | flops 4339086336 | bytes 34697220 | tf_op jit(solution)/shard_map/td,qjd->qjt/dot_general | solution.py:48
  458.9 0.1 reduce_sum.18
  459.0 12.3 %psum.7 = f32[6,4]{0,1:T(4,128)S(1)} all-reduce(f32[6,4]{0,1:T(4,128)S(1)} %bitcast.25), channel_id=1, replica_groups=mesh['dp'=4,'tensor'=8] {'tensor'}, use_global_device_ids=true, to_apply=%region_2.3 | all-reduce | flops 24 | bytes 192 | tf_op jit(solution)/shard_map/psum | solution.py:58
  471.2 0.6 broadcast_multiply_fusion
  (10 shorter events, 0.0 us)
Async XLA Ops:
  6.5 52.0 %all-gather.4.cloned.1.call-start = ((), (), s32[]{:S(2)}) async-start(), calls=%async_computation | async-start | bytes 7077888 | tf_op jit(solution)/shard_map/all_gather | solution.py:8
  7.3 194.9 %all-gather.8.cloned.1.call-start = ((), (), s32[]{:S(2)}) async-start(), calls=%async_computation.2 | async-start | bytes 9510912 | tf_op jit(solution)/shard_map/all_gather | solution.py:15
  8.0 59.5 %copy-start = (f32[688,1024]{1,0:T(8,128)S(1)}, f32[688,1024]{1,0:T(8,128)}, u32[]{:S(2)}) copy-start(f32[688,1024]{1,0:T(8,128)} %param.13) | copy-start | bytes 8454148
  8.0 205.0 %all-gather.6.cloned.1.call-start = ((), (), s32[]{:S(2)}) async-start(), calls=%async_computation.1 | async-start | bytes 7077888 | tf_op jit(solution)/shard_map/all_gather | solution.py:10
  68.0 134.0 %copy-start.1 = (s32[6]{0:T(128)S(1)}, s32[6]{0:T(128)}, u32[]{:S(2)}) copy-start(s32[6]{0:T(128)} %param.15) | copy-start | bytes 76
  75.5 126.5 %collective-permute-start.1 = (bf16[4,688,1024]{2,1,0:T(8,128)(2,1)}, bf16[4,688,1024]{2,1,0:T(8,128)(2,1)}, u32[]{:S(2)}, u32[]{:S(2)}) collective-permute-start(bf16[4,688,1024]{2,1,0:T(8,128)(2,1)} %divide_convert_fusion), channel_id=1, source_target_pairs={{0,8},{8,16},{16,24},{24,0},{1,9},{9,17},{17,25},{25,1},{2,10},{10... | collective-permute-start | bytes 16908296 | tf_op jit(solution)/shard_map/ppermute | solution.py:37
  77.1 244.5 %collective-permute-start = (bf16[4,688,1024]{2,1,0:T(8,128)(2,1)}, bf16[4,688,1024]{2,1,0:T(8,128)(2,1)}, u32[]{:S(2)}, u32[]{:S(2)}) collective-permute-start(bf16[4,688,1024]{2,1,0:T(8,128)(2,1)} %divide_convert_fusion), channel_id=1, source_target_pairs={{0,24},{8,0},{16,8},{24,16},{1,25},{9,1},{17,9},{25,17},{2,26},{10... | collective-permute-start | bytes 16908296 | tf_op jit(solution)/shard_map/ppermute | solution.py:39
  202.0 240.9 %collective-permute-start.2 = (bf16[4,688,1024]{2,1,0:T(8,128)(2,1)}, bf16[4,688,1024]{2,1,0:T(8,128)(2,1)}, u32[]{:S(2)}, u32[]{:S(2)}) collective-permute-start(bf16[4,688,1024]{2,1,0:T(8,128)(2,1)} %collective-permute-done.1), channel_id=1, source_target_pairs={{0,8},{8,16},{16,24},{24,0},{1,9},{9,17},{17,25},{25,1},{2,10},{10... | collective-permute-start | bytes 16908296 | tf_op jit(solution)/shard_map/ppermute | solution.py:37
  213.1 11.1 %copy-start.2 = (bf16[768,4096]{1,0:T(8,128)(2,1)S(1)}, bf16[768,4096]{1,0:T(8,128)(2,1)}, u32[]{:S(2)}) copy-start(bf16[768,4096]{1,0:T(8,128)(2,1)} %all-gather.6.cloned.1.call-done) | copy-start | bytes 18874372
Sparse Core Ops, SparseCore 0:
  9.2 49.2 all-gather.3
  60.4 54.5 all-gather.7
  116.9 46.5 all-gather.5
